TPU v7x, 512 devices: a whole 4x8x8 slice. The times are simulated.
512 devices in a mesh: req: 64 (over x, y, core), head: 8 (over z).
Axes of the slice: x: 4, y: 8, z: 8, core: 2. Of those that a mesh axis runs over, the one named last changes fastest.
Arguments:
- hidden: bfloat16 [512, 4096], P(None, 'req'), may hold values from -16 to 16
- query_key_value_weight: bfloat16 [4096, 8, 768], P('req', 'head'), may hold values from -0.1875 to 0.1875
- output_weight: bfloat16 [4096, 4096], P('head', 'req'), may hold values from -0.375 to 0.375
- kv_pool: bfloat16 [4096, 8, 128, 256], P('req', 'head'), may hold values from -68 to 68
- lengths: int32 [512], P('req'), may hold values from 513 to 2048, as said below
- page_table: int32 [512, 16], P('req'), may hold values from 0 to 127, as said below
- send_slots: int32 [4096], P('req'), may hold values from 0 to 63, as said below
Outputs:
- attn_out: bfloat16 [512, 4096], P('head', 'req')
Inputs may be any that keep to these rules, and one draw needn't show every extreme that they name: `page_table`: A request's live positions name distinct slots of its group's store, and every other entry is 0. Slots below 64 are the group's own pool rows; slot 64 + s is the page that group s sends to it. Every group uses exactly 32 of the 64 pages sent to it, never for a long request. `send_slots`: every group sends one page to every group; rows whose page the receiver does not use name an arbitrary slot. In 16 of the groups one request is long (more than (15) * 128 tokens); all others hold at most 768 tokens. The new token sits at position lengths[r].
All inputs are finite; a program needn't handle non-finite values.
Results may differ from a plain program's by a relative error of at most 0.018.
Values may be sent and summed in bfloat16 or wider, within the bound.
A program may use at most 64 MiB of HBM per device.

v0:
```python
import jax
import jax.numpy as jnp
from jax import lax
from jax.sharding import PartitionSpec as P

ROPE_BASE = 500000.0
NEG_FILL = -1e30


def rotate(vectors, angles):
    half_width = vectors.shape[-1] // 2
    first_half = vectors[..., :half_width]
    second_half = vectors[..., half_width:]
    cosine = jnp.cos(angles)
    sine_part = jnp.sin(angles)
    return jnp.concatenate(
        [
            first_half * cosine - second_half * sine_part,
            second_half * cosine + first_half * sine_part,
        ],
        axis=-1,
    )


def rope_angles(lengths, width):
    exponent = jnp.arange(width // 2, dtype=jnp.float32) * (2.0 / width)
    inverse = 1.0 / ROPE_BASE**exponent
    return lengths.astype(jnp.float32)[:, None] * inverse[None, :]


def split_projection(projected_rows, lengths):
    angles = rope_angles(lengths, projected_rows.shape[-1])
    queries = rotate(projected_rows[:, :, :-2], angles[:, None, None, :]).astype(jnp.bfloat16)
    new_keys = rotate(projected_rows[:, :, -2], angles[:, None, :]).astype(jnp.bfloat16)
    new_values = projected_rows[:, :, -1].astype(jnp.bfloat16)
    return (queries, new_keys, new_values)


def page_stats(queries, pages, valid_tokens, score_scale):
    head_dim = pages.shape[-1] // 2
    scores = (
        jnp.einsum(
            "nhqd,nhtd->nhqt", queries, pages[..., :head_dim], preferred_element_type=jnp.float32
        )
        * score_scale
    )
    token_mask = jnp.arange(pages.shape[2])[None, None, None, :] < valid_tokens[:, None, None, None]
    masked = jnp.where(token_mask, scores, NEG_FILL)
    top_score = jnp.max(masked, axis=-1)
    weights = jnp.where(token_mask, jnp.exp(scores - top_score[..., None]), 0.0)
    weight_sum = jnp.sum(weights, axis=-1)
    weighted_values = jnp.einsum(
        "nhqt,nhtd->nhqd",
        weights.astype(jnp.bfloat16),
        pages[..., head_dim:],
        preferred_element_type=jnp.float32,
    )
    return (top_score, weight_sum, weighted_values)


def shards(hidden, query_key_value_weight, output_weight, kv_pool, lengths, page_table, send_slots):
    groups = lax.axis_size("req")
    local_count = lengths.shape[0]
    head_count = query_key_value_weight.shape[1]
    pool_slots = kv_pool.shape[0]
    page_len = kv_pool.shape[2]
    head_dim = kv_pool.shape[3] // 2
    per_head = query_key_value_weight.shape[2] // head_dim
    flat_weight = query_key_value_weight.reshape(
        query_key_value_weight.shape[0], head_count * per_head * head_dim
    )
    projected_rows = lax.psum_scatter(
        jnp.dot(hidden, flat_weight, preferred_element_type=jnp.float32),
        "req",
        scatter_dimension=0,
        tiled=True,
    )
    projected_rows = projected_rows.reshape(local_count, head_count, per_head, head_dim)
    queries, new_keys, new_values = split_projection(projected_rows, lengths)
    score_scale = head_dim ** (-0.5)
    self_scores = (
        jnp.sum(queries.astype(jnp.float32) * new_keys.astype(jnp.float32)[:, :, None, :], axis=-1)
        * score_scale
    )
    total_slots = pool_slots + groups
    places = jnp.arange(page_table.shape[1], dtype=jnp.int32)
    is_live = places[None, :] * page_len < lengths[:, None]
    tokens_in = jnp.clip(lengths[:, None] - places[None, :] * page_len, 0, page_len)
    table_hits = (
        page_table[:, :, None] == jnp.arange(total_slots, dtype=jnp.int32)[None, None, :]
    ) & is_live[:, :, None]
    owner_map = jnp.any(table_hits, axis=1).T
    valid_tokens = jnp.sum(jnp.where(table_hits, tokens_in[:, :, None], 0), axis=(0, 1))
    owner_index = jnp.sum(
        jnp.where(owner_map, jnp.arange(local_count, dtype=jnp.int32)[None, :], 0), axis=1
    )
    slot_queries = jnp.einsum(
        "nr,rhqd->nhqd", owner_map.astype(jnp.bfloat16), queries, preferred_element_type=jnp.float32
    ).astype(jnp.bfloat16)
    outgoing = kv_pool[send_slots]
    arrived = lax.all_to_all(outgoing, "req", split_axis=0, concat_axis=0, tiled=True)
    page_store = jnp.concatenate([kv_pool, arrived], axis=0)
    page_max, page_sum, page_acc = page_stats(slot_queries, page_store, valid_tokens, score_scale)
    owned_max = jnp.max(jnp.where(owner_map[:, :, None, None], page_max[:, None], NEG_FILL), axis=0)
    top_score = jnp.maximum(owned_max, self_scores)
    factors = jnp.exp(page_max - top_score[owner_index])
    owner_float = owner_map.astype(jnp.float32)
    self_weight = jnp.exp(self_scores - top_score)
    total_weight_sum = (
        jnp.einsum("nr,nhq->rhq", owner_float, factors * page_sum, precision=lax.Precision.HIGHEST)
        + self_weight
    )
    weighted_values = jnp.einsum(
        "nr,nhqd->rhqd", owner_float, factors[..., None] * page_acc, precision=lax.Precision.HIGHEST
    )
    weighted_values = (
        weighted_values + self_weight[..., None] * new_values.astype(jnp.float32)[:, :, None, :]
    )
    output_per_head = (
        (weighted_values / total_weight_sum[..., None])
        .astype(jnp.bfloat16)
        .reshape(local_count, head_count * (per_head - 2) * head_dim)
    )
    partial_out = jnp.dot(
        lax.all_gather(output_per_head, "req", axis=0, tiled=True),
        output_weight,
        preferred_element_type=jnp.float32,
    )
    return lax.psum_scatter(
        partial_out.astype(jnp.bfloat16), "head", scatter_dimension=0, tiled=True
    )


def solution(mesh):
    return jax.shard_map(
        shards,
        mesh=mesh,
        in_specs=(
            P(None, "req"),
            P("req", "head", None),
            P("head", "req"),
            P("req", "head", None, None),
            P("req"),
            P("req", None),
            P("req"),
        ),
        out_specs=P("head", "req"),
        check_vma=False,
    )
```

profile of v0, /device:TPU:7, one launch (start us, length us, event | category | flops | bytes accessed | tf_op | source)
XLA Modules:
  0.0 285.7 jit_solution(14235447509010207527)
XLA Ops:
  6.5 0.0 copy-start
  6.5 0.7 compare_select_fusion.1
  7.2 5.0 %gather_fusion = bf16[64,128,256]{2,1,0:T(8,128)(2,1)} fusion(bf16[64,128,256]{2,1,0:T(8,128)(2,1)} %bitcast.50, s32[1024]{0:T(1024)S(1)} %pad_clamp_fusion.1), kind=kCustom, calls=%fused_computation | custom fusion | bytes 8388864 | tf_op jit(solution)/shard_map/gather | solution.py:100
  12.2 0.0 copy-start.2
  12.2 0.0 copy-start.4
  12.2 0.0 copy-start.3
  12.2 11.6 %all-to-all-start = ((bf16[64,1,128,256]{3,2,1,0:T(8,128)(2,1)}), bf16[64,1,128,256]{3,2,1,0:T(8,128)(2,1)}, u32[]{:S(2)}, u32[]{:S(2)}) async-start(bf16[64,1,128,256]{3,2,1,0:T(8,128)(2,1)} %bitcast.53), calls=%async_computation.1 | async-start | bytes 8388608 | tf_op jit(solution)/shard_map/all_to_all | solution.py:101
  23.8 0.0 reduce-scatter.3.cloned.1.call-start
  23.9 0.0 copy-done
  23.9 0.0 copy-done.2
  23.9 1.6 fusion.25
  25.5 0.0 reduce-scatter.3.cloned.1.call-update
  25.5 0.0 reduce-scatter.5.cloned.1.call-start
  25.6 0.0 copy-done.4
  25.6 0.1 broadcast_compare_fusion
  25.7 0.0 copy-done.3
  25.7 0.1 fusion.29
  25.8 0.1 subtract_clamp_fusion
  25.9 0.1 select_reduce_fusion.1
  26.1 0.1 multiply_cosine_fusion.1
  26.2 0.1 iota_compare_fusion
  26.3 149.6 %reduce-scatter.3.cloned.1.call-done = f32[8,768]{1,0:T(8,128)} async-done(((f32[512,768]{1,0:T(8,128)}), f32[8,768]{1,0:T(8,128)}) %reduce-scatter.3.cloned.1.call-update) | async-done | bytes 24592 | tf_op jit(solution)/shard_map/reduce_scatter | solution.py:72
  175.8 0.7 slice_bitcast_fusion
  176.5 0.1 fusion.46
  176.6 0.1 maximum_convert_fusion
  176.7 0.9 subtract_convert_fusion
  177.6 0.2 multiply_reduce_fusion
  177.8 0.7 fusion.44
  178.4 0.3 convolution_convert_fusion.1
  178.7 0.0 all-to-all-done
  178.7 4.6 %select_reduce_fusion = (f32[128,4]{1,0:T(8,128)S(1)}, f32[128,4,128]{2,1,0:T(4,128)S(1)}) fusion(pred[128,128]{1,0:T(8,128)(4,1)S(1)} %iota_compare_fusion, bf16[64,1,128,256]{3,2,0,1:T(8,128)(2,1)} %bitcast.51, bf16[64,1,128,256]{3,2,0,1:T(8,128)(2,1)} %bitcast.8, bf16[128,4,128]{2,0,1:T(8,128)(2,1)S(1)} %convolution_convert_fusion.1), kind=kOutput, calls=%fused_computation.22 | convolution fusion | flops 19070464 | bytes 8800256 | tf_op jit(solution)/shard_map/nhqd,nhtd->nhqt/dot_general | solution.py:42
  183.3 0.1 copy.20
  183.4 0.1 select_reduce_fusion.2
  183.5 0.1 copy.21
  183.6 0.7 gather_fusion.1
  184.3 0.4 fusion.18
  184.6 0.0 copy-start.1
  184.7 3.5 %fusion.11 = f32[128,4,128]{2,1,0:T(4,128)S(1)} fusion(bf16[64,1,128,256]{3,2,0,1:T(8,128)(2,1)} %bitcast.8, bf16[64,1,128,256]{3,2,0,1:T(8,128)(2,1)} %bitcast.52, f32[128,4,128]{2,1,0:T(4,128)S(1)} %get-tuple-element.14, f32[128,4]{1,0:T(8,128)S(1)} %get-tuple-element.13, f32[128,4]{1,0:T(8,128)S(1)} %subtract_exponential_fusion, ...), kind=kOutput, calls=%fused_computation.12 | convolution fusion | flops 25427968 | bytes 8933376 | tf_op jit(solution)/shard_map/nhqt,nhtd->nhqd/dot_general | solution.py:52
  188.2 0.2 convolution_add_fusion.1
  188.4 0.2 fusion.16
  188.6 54.3 %all_gather.3 = bf16[512,512]{1,0:T(8,128)(2,1)S(1)} all-gather(bf16[8,512]{1,0:T(8,128)(2,1)S(1)} %fusion.16), channel_id=1, replica_groups=mesh['req'=64,'head'=8] {'req'}, dimensions={0}, use_global_device_ids=true | all-gather | bytes 532480 | tf_op jit(solution)/shard_map/all_gather | solution.py:125
  243.0 0.0 copy-done.1
  243.0 0.9 convolution_convert_fusion
  243.9 0.0 reduce-scatter.5.cloned.1.call-update
  243.9 34.9 %reduce-scatter.5.cloned.1.call-done = bf16[64,64]{1,0:T(8,128)(2,1)} async-done(((bf16[512,64]{1,0:T(8,128)(2,1)}), bf16[64,64]{1,0:T(8,128)(2,1)}) %reduce-scatter.5.cloned.1.call-update) | async-done | bytes 8208 | tf_op jit(solution)/shard_map/reduce_scatter | solution.py:129
  (9 shorter events, 0.1 us)
Async XLA Ops:
  6.5 17.3 %copy-start = (bf16[64,1,768]{2,0,1:T(8,128)(2,1)S(1)}, bf16[64,1,768]{2,0,1:T(8,128)(2,1)}, u32[]{:S(2)}) copy-start(bf16[64,1,768]{2,0,1:T(8,128)(2,1)} %param.8) | copy-start | bytes 294916
  12.2 11.7 %copy-start.2 = (bf16[512,64]{0,1:T(8,128)(2,1)S(1)}, bf16[512,64]{0,1:T(8,128)(2,1)}, u32[]{:S(2)}) copy-start(bf16[512,64]{0,1:T(8,128)(2,1)} %param.7) | copy-start | bytes 196612
  12.2 13.4 %copy-start.4 = (s32[8]{0:T(128)S(1)}, s32[8]{0:T(128)}, u32[]{:S(2)}) copy-start(s32[8]{0:T(128)} %param.11) | copy-start | bytes 100
  12.2 13.5 %copy-start.3 = (s32[8,16]{1,0:T(8,128)S(1)}, s32[8,16]{1,0:T(8,128)}, u32[]{:S(2)}) copy-start(s32[8,16]{1,0:T(8,128)} %param.12) | copy-start | bytes 1540
  12.2 166.5 %all-to-all-start = ((bf16[64,1,128,256]{3,2,1,0:T(8,128)(2,1)}), bf16[64,1,128,256]{3,2,1,0:T(8,128)(2,1)}, u32[]{:S(2)}, u32[]{:S(2)}) async-start(bf16[64,1,128,256]{3,2,1,0:T(8,128)(2,1)} %bitcast.53), calls=%async_computation.1 | async-start | bytes 8388608 | tf_op jit(solution)/shard_map/all_to_all | solution.py:101
  23.8 152.0 %reduce-scatter.3.cloned.1.call-start = ((), (), s32[]{:S(2)}) async-start(), calls=%async_computation.3 | async-start | bytes 1597440 | tf_op jit(solution)/shard_map/reduce_scatter | solution.py:72
  25.5 253.3 %reduce-scatter.5.cloned.1.call-start = ((), (), s32[]{:S(2)}) async-start(), calls=%async_computation.4 | async-start | bytes 147456 | tf_op jit(solution)/shard_map/reduce_scatter | solution.py:129
  184.6 58.3 %copy-start.1 = (bf16[512,64]{0,1:T(8,128)(2,1)S(1)}, bf16[512,64]{0,1:T(8,128)(2,1)}, u32[]{:S(2)}) copy-start(bf16[512,64]{0,1:T(8,128)(2,1)} %param.9) | copy-start | bytes 196612
Sparse Core Ops, SparseCore 0:
  29.2 146.5 reduce-scatter.2
  244.0 34.7 reduce-scatter.4
where the time goes:
time: 292 us; the launch traced here: 286 us
  waiting for transfers between devices  185 us (63%)
  blocking collectives  54.3 us (19%)
  between operations  13.5 us (5%)
  starting transfers between devices  11.7 us (4%)
  matrix products  11.3 us (4%)
  local copies, waits for them, and re-layouts  6.47 us (2%)
  other arithmetic  3.76 us (1%)
    reduce_scatter x1, waiting for transfers between devices, shards(): lax.psum_scatter(jnp.dot(hidden, flat_weight, preferred_element_type=jnp....  150 us
    all_gather x1, blocking collectives, shards(): lax.all_gather(output_per_head, 'req', axis=0, tiled=True)  54.3 us
    reduce_scatter x1, waiting for transfers between devices, shards(): lax.psum_scatter(partial_out.astype(jnp.bfloat16), 'head', scatter_dimens...  34.9 us
    all_to_all x1, starting transfers between devices, shards(): lax.all_to_all(outgoing, 'req', split_axis=0, concat_axis=0, tiled=True)  11.6 us
  transfers between devices with their start and end apart: 3, of which 2 were waited for; matrix products, arithmetic and copies ran while one was open for 2% of the time, Pallas kernels for 0%

commit v1 on v0

v1 whole, which is shorter than its diff:
```python
import jax
import jax.numpy as jnp
from jax import lax
from jax.experimental import pallas as pl
from jax.experimental.pallas import tpu as pltpu
from jax.sharding import PartitionSpec as P

ROPE_BASE = 500000.0
NEG_FILL = -1e30
SCALE = 128 ** (-0.5)


def rotate(vectors, angles):
    half_width = vectors.shape[-1] // 2
    first_half = vectors[..., :half_width]
    second_half = vectors[..., half_width:]
    cosine = jnp.cos(angles)
    sine_part = jnp.sin(angles)
    return jnp.concatenate(
        [
            first_half * cosine - second_half * sine_part,
            second_half * cosine + first_half * sine_part,
        ],
        axis=-1,
    )


def rope_angles(lengths, width):
    exponent = jnp.arange(width // 2, dtype=jnp.float32) * (2.0 / width)
    inverse = 1.0 / ROPE_BASE**exponent
    return lengths.astype(jnp.float32)[:, None] * inverse[None, :]


def remote(src, dst, send, recv, req, head=None):
    where = {"req": req} if head is None else {"req": req, "head": head}
    return pltpu.make_async_remote_copy(
        src_ref=src, dst_ref=dst, send_sem=send, recv_sem=recv,
        device_id=where, device_id_type=pl.DeviceIdType.MESH,
    )


def greet(barrier, req, head=None):
    where = {"req": req} if head is None else {"req": req, "head": head}
    pl.semaphore_signal(barrier, inc=1, device_id=where, device_id_type=pl.DeviceIdType.MESH)


def for_each(start, stop, body):
    def step(i, carry):
        body(i)
        return carry
    lax.fori_loop(start, stop, step, 0)


def place(req):
    return req // 16, lax.rem(req // 2, 8), lax.rem(req, 2)


def project_kernel(
    pay_ref, wo_ref, out_ref, wg_ref, gathered, partial, parts, s1, r1, s2, r2, s3, r3, own
):
    req = lax.axis_index("req")
    x, y, c = place(req)
    xc = x * 2 + c
    yc = y * 2 + c

    def at_xc(i):
        return (i // 2) * 16 + y * 2 + lax.rem(i, 2)

    barrier = pltpu.get_barrier_semaphore()
    for_each(1, 8, lambda k: greet(barrier, at_xc(lax.rem(xc + k, 8))))
    for_each(1, 16, lambda k: greet(barrier, x * 16 + lax.rem(yc + k, 16)))
    own_pay = pltpu.make_async_copy(pay_ref.at[xc], gathered.at[xc], own.at[0])
    own_wo = pltpu.make_async_copy(wo_ref, wg_ref.at[xc], own.at[1])
    own_pay.start()
    own_wo.start()
    pl.semaphore_wait(barrier, 22)

    def send_pay(k):
        peer = lax.rem(xc + k, 8)
        return remote(pay_ref.at[peer], gathered.at[xc], s1.at[k], r1.at[k], at_xc(peer))

    def send_wo(k):
        peer = lax.rem(xc + k, 8)
        return remote(wo_ref, wg_ref.at[xc], s3.at[k], r3.at[k], at_xc(peer))

    def send_part(k):
        peer = lax.rem(yc + k, 16)
        return remote(partial.at[peer], parts.at[yc], s2.at[k], r2.at[k], x * 16 + peer)

    for_each(1, 8, lambda k: send_pay(k).start())
    own_pay.wait()
    for_each(1, 8, lambda k: send_pay(k).wait_recv())
    for_each(1, 8, lambda k: send_wo(k).start())
    rows = gathered[:, :, :128].reshape(512, 128)
    cols = gathered[:, :, 128:].reshape(512, 384)
    sums = lax.dot_general(
        rows, cols, (((0,), (0,)), ((), ())), preferred_element_type=jnp.float32
    )
    partial[...] = sums.reshape(16, 8, 384)
    own_part = pltpu.make_async_copy(partial.at[yc], parts.at[yc], own.at[0])
    own_part.start()
    for_each(1, 16, lambda k: send_part(k).start())
    own_part.wait()
    for_each(1, 16, lambda k: send_part(k).wait_recv())
    total = parts[0:2]
    for i in range(1, 8):
        total = total + parts[2 * i : 2 * i + 2]
    out_ref[...] = total
    own_wo.wait()
    for_each(1, 8, lambda k: send_pay(k).wait_send())
    for_each(1, 16, lambda k: send_part(k).wait_send())
    for_each(1, 8, lambda k: send_wo(k).wait())


def split_three(v):
    high = v.astype(jnp.bfloat16).astype(jnp.float32)
    rest = v - high
    mid = rest.astype(jnp.bfloat16).astype(jnp.float32)
    return high, mid, rest - mid


def attend_kernel(
    slots_ref, msg_ref, q_ref, valid_ref, kv_ref, back_ref, acc_ref, max_ref, sum_ref,
    pages, asked, scores, reply, s1, r1, s2, r2, own,
):
    me = lax.axis_index("req")
    load = pltpu.make_async_copy(kv_ref, pages, own.at[0])
    load.start()
    barrier = pltpu.get_barrier_semaphore()
    for_each(1, 64, lambda k: greet(barrier, lax.rem(me + k, 64)))
    own_ask = pltpu.make_async_copy(msg_ref.at[me], asked.at[me], own.at[1])
    own_ask.start()
    pl.semaphore_wait(barrier, 63)

    def ask(k):
        peer = lax.rem(me + k, 64)
        return remote(msg_ref.at[peer], asked.at[me], s1.at[k], r1.at[k], peer)

    def answer(k):
        peer = lax.rem(me + k, 64)
        return remote(reply.at[peer], back_ref.at[me], s2.at[k], r2.at[k], peer)

    for_each(1, 64, lambda k: ask(k).start())
    load.wait()

    lane = lax.broadcasted_iota(jnp.int32, (32, 128), 1)
    queries = q_ref[...]
    valid = valid_ref[...]

    def score(e, top):
        s = lax.dot_general(
            queries, pages[e, :, 0:128], (((1,), (1,)), ((), ())),
            preferred_element_type=jnp.float32,
        ) * SCALE
        tokens = jnp.sum(jnp.where(lane == e, valid, 0), axis=1, keepdims=True)
        s = jnp.where(lane < tokens, s, NEG_FILL)
        scores[e] = s
        return jnp.maximum(top, s)

    top = lax.fori_loop(0, 64, score, jnp.full((32, 128), NEG_FILL, jnp.float32), unroll=4)
    top = jnp.broadcast_to(jnp.max(top, axis=1, keepdims=True), (32, 128))

    def gather(e, carry):
        acc, total = carry
        s = scores[e]
        w = jnp.where(s > 0.5 * NEG_FILL, jnp.exp(s - top), 0.0)
        acc = acc + jnp.dot(
            w.astype(jnp.bfloat16), pages[e, :, 128:256], preferred_element_type=jnp.float32
        )
        return acc, total + w

    zero = jnp.zeros((32, 128), jnp.float32)
    acc, total = lax.fori_loop(0, 64, gather, (zero, zero), unroll=4)
    acc_ref[...] = acc
    max_ref[...] = top
    sum_ref[...] = jnp.broadcast_to(jnp.sum(total, axis=1, keepdims=True), (32, 128))

    own_ask.wait()
    for_each(1, 64, lambda k: ask(k).wait_recv())

    lane8 = lax.broadcasted_iota(jnp.int32, (8, 128), 1)
    row8 = lax.broadcasted_iota(jnp.int32, (8, 128), 0)

    def serve(g, carry):
        slot = slots_ref[g]
        query = asked[g].astype(jnp.float32)
        tokens = query[4:5, 0:1]
        query = jnp.where(row8 < 4, query, pltpu.roll(query, 4, 0)).astype(jnp.bfloat16)
        s = lax.dot_general(
            query, pages[slot, :, 0:128], (((1,), (1,)), ((), ())),
            preferred_element_type=jnp.float32,
        ) * SCALE
        mask = lane8.astype(jnp.float32) < tokens
        s = jnp.where(mask, s, NEG_FILL)
        m = jnp.max(s, axis=1, keepdims=True)
        w = jnp.where(mask, jnp.exp(s - m), 0.0)
        l = jnp.sum(w, axis=1, keepdims=True)
        a = jnp.dot(
            w.astype(jnp.bfloat16), pages[slot, :, 128:256], preferred_element_type=jnp.float32
        )
        m0, m1, m2 = split_three(jnp.broadcast_to(m, (8, 128)))
        l0, l1, l2 = split_three(jnp.broadcast_to(l, (8, 128)))
        stats = jnp.where(lane8 < 16, m0, jnp.where(lane8 < 32, m1, jnp.where(lane8 < 48, m2,
                jnp.where(lane8 < 64, l0, jnp.where(lane8 < 80, l1, l2)))))
        reply[g] = jnp.where(row8 < 4, a, stats).astype(jnp.bfloat16)
        return carry

    lax.fori_loop(0, 64, serve, 0, unroll=4)
    own_answer = pltpu.make_async_copy(reply.at[me], back_ref.at[me], own.at[0])
    own_answer.start()
    for_each(1, 64, lambda k: answer(k).start())
    own_answer.wait()
    for_each(1, 64, lambda k: answer(k).wait_recv())
    for_each(1, 64, lambda k: ask(k).wait_send())
    for_each(1, 64, lambda k: answer(k).wait_send())


def output_kernel(heads_ref, wg_ref, out_ref, rows, partial, parts, s1, r1, s2, r2, own):
    req = lax.axis_index("req")
    z = lax.axis_index("head")
    x, y, c = place(req)
    mine = (z // 2) == x

    def dest(k):
        return (k // 4) * 16 + y * 2 + lax.rem(k // 2, 2), x * 2 + lax.rem(k, 2)

    def origin(k):
        return (z // 2) * 16 + y * 2 + k // 8, lax.rem(k, 8)

    def is_me(pair):
        return jnp.logical_and(pair[0] == req, pair[1] == z)

    barrier = pltpu.get_barrier_semaphore()
    for_each(1, 8, lambda k: greet(barrier, x * 16 + lax.rem(y + k, 8) * 2 + c))

    def hello(k):
        @pl.when(jnp.logical_not(is_me(origin(k))))
        def _():
            greet(barrier, *origin(k))

    for_each(0, 16, hello)
    own_rows = pltpu.make_async_copy(heads_ref, rows.at[y], own.at[0])
    own_rows.start()

    @pl.when(mine)
    def _():
        pl.semaphore_wait(barrier, 22)

    @pl.when(jnp.logical_not(mine))
    def _():
        pl.semaphore_wait(barrier, 23)

    def send_rows(k):
        peer = x * 16 + lax.rem(y + k, 8) * 2 + c
        return remote(heads_ref, rows.at[y], s1.at[k], r1.at[k], peer)

    for_each(1, 8, lambda k: send_rows(k).start())
    own_rows.wait()
    for_each(1, 8, lambda k: send_rows(k).wait_recv())
    heads = rows[...].astype(jnp.float32).reshape(64, 512).astype(jnp.bfloat16)
    for i in range(8):
        tile = lax.dot_general(
            heads, wg_ref[i], (((1,), (1,)), ((), ())), preferred_element_type=jnp.float32
        ).astype(jnp.bfloat16)
        partial[2 * i] = tile[0:32]
        partial[2 * i + 1] = tile[32:64]

    spot = c * 8 + z

    def push(k):
        return remote(partial.at[k], parts.at[spot], s2.at[k], r2.at[spot], *dest(k))

    def send(k):
        @pl.when(is_me(dest(k)))
        def _():
            pltpu.make_async_copy(partial.at[k], parts.at[spot], r2.at[spot]).start()

        @pl.when(jnp.logical_not(is_me(dest(k))))
        def _():
            push(k).start()

    for_each(0, 16, send)

    def receive(k):
        pltpu.make_async_copy(parts.at[k], parts.at[k], r2.at[k]).wait()

    for_each(0, 16, receive)
    for j in range(2):
        total = parts[8 * j].astype(jnp.float32)
        for h in range(1, 8):
            total = total + parts[8 * j + h].astype(jnp.float32)
        out_ref[j] = total
    for_each(1, 8, lambda k: send_rows(k).wait_send())

    def sent(k):
        @pl.when(jnp.logical_not(is_me(dest(k))))
        def _():
            push(k).wait_send()

    for_each(0, 16, sent)


def vmem():
    return pl.BlockSpec(memory_space=pltpu.VMEM)


def params(ident):
    return pltpu.CompilerParams(collective_id=ident, has_side_effects=True)


def dma(count):
    return pltpu.SemaphoreType.DMA((count,))


def shards(hidden, query_key_value_weight, output_weight, kv_pool, lengths, page_table, send_slots):
    bf16, f32 = jnp.bfloat16, jnp.float32
    hidden_t = hidden.T.reshape(64, 4, 128).transpose(1, 0, 2)
    weight = query_key_value_weight.reshape(64, 2, 384).transpose(1, 0, 2)
    payload = jnp.concatenate(
        [
            jnp.broadcast_to(hidden_t[:, None], (4, 2, 64, 128)),
            jnp.broadcast_to(weight[None], (4, 2, 64, 384)),
        ],
        axis=-1,
    ).reshape(8, 64, 512)
    projected, out_cols = pl.pallas_call(
        project_kernel,
        out_shape=(
            jax.ShapeDtypeStruct((2, 8, 384), f32),
            jax.ShapeDtypeStruct((8, 64, 512), bf16),
        ),
        in_specs=[vmem()] * 2,
        out_specs=(vmem(), vmem()),
        scratch_shapes=[
            pltpu.VMEM((8, 64, 512), bf16),
            pltpu.VMEM((16, 8, 384), f32),
            pltpu.VMEM((16, 8, 384), f32),
            dma(8), dma(8), dma(16), dma(16), dma(8), dma(8), dma(2),
        ],
        compiler_params=params(1),
    )(payload, output_weight.T)

    rows = projected.transpose(1, 0, 2).reshape(8, 6, 128)
    angles = rope_angles(lengths, 128)
    queries = rotate(rows[:, :4], angles[:, None, :]).astype(bf16)
    new_keys = rotate(rows[:, 4], angles).astype(bf16)
    new_values = rows[:, 5].astype(bf16)
    self_scores = (
        jnp.sum(queries.astype(f32) * new_keys.astype(f32)[:, None, :], axis=-1) * SCALE
    )

    places = jnp.arange(16, dtype=jnp.int32)
    is_live = places[None, :] * 128 < lengths[:, None]
    tokens_in = jnp.clip(lengths[:, None] - places[None, :] * 128, 0, 128)
    hits = (page_table[:, :, None] == jnp.arange(128, dtype=jnp.int32)) & is_live[:, :, None]
    valid = jnp.sum(jnp.where(hits, tokens_in[:, :, None], 0), axis=1)
    owned = valid[:, 64:] > 0
    asking = jnp.einsum(
        "rs,rqd->sqd", owned.astype(bf16), queries, preferred_element_type=f32
    ).astype(bf16)
    tokens = jnp.sum(valid[:, 64:], axis=0).astype(bf16)
    message = jnp.concatenate(
        [asking, jnp.broadcast_to(tokens[:, None, None], (64, 4, 128))], axis=1
    )
    back, acc, top, total = pl.pallas_call(
        attend_kernel,
        out_shape=(
            jax.ShapeDtypeStruct((64, 8, 128), bf16),
            jax.ShapeDtypeStruct((32, 128), f32),
            jax.ShapeDtypeStruct((32, 128), f32),
            jax.ShapeDtypeStruct((32, 128), f32),
        ),
        in_specs=[
            pl.BlockSpec(memory_space=pltpu.SMEM), vmem(), vmem(), vmem(),
            pl.BlockSpec(memory_space=pl.ANY),
        ],
        out_specs=(vmem(), vmem(), vmem(), vmem()),
        scratch_shapes=[
            pltpu.VMEM((64, 128, 256), bf16),
            pltpu.VMEM((64, 8, 128), bf16),
            pltpu.VMEM((64, 32, 128), f32),
            pltpu.VMEM((64, 8, 128), bf16),
            dma(64), dma(64), dma(64), dma(64), dma(2),
        ],
        compiler_params=params(2),
    )(
        send_slots, message, queries.transpose(1, 0, 2).reshape(32, 128),
        jnp.tile(valid, (4, 1)), kv_pool.reshape(64, 128, 256),
    )

    far = back[:, :4].astype(f32)
    stats = back[:, 4:].astype(f32)
    far_max = stats[:, :, 0] + stats[:, :, 16] + stats[:, :, 32]
    far_sum = stats[:, :, 48] + stats[:, :, 64] + stats[:, :, 80]
    near = acc.reshape(4, 8, 128).transpose(1, 0, 2)
    near_max = top[:, 0].reshape(4, 8).T
    near_sum = total[:, 0].reshape(4, 8).T
    picked = owned[:, :, None]
    peak = jnp.max(jnp.where(picked, far_max[None], NEG_FILL), axis=1)
    peak = jnp.maximum(jnp.maximum(peak, near_max), self_scores)
    factors = jnp.where(picked, jnp.exp(jnp.minimum(far_max[None] - peak[:, None], 0.0)), 0.0)
    near_factor = jnp.exp(near_max - peak)
    self_factor = jnp.exp(self_scores - peak)
    weight_sum = jnp.sum(factors * far_sum[None], axis=1) + near_factor * near_sum + self_factor
    weighted = (
        jnp.einsum("rsq,sqd->rqd", factors, far, precision=lax.Precision.HIGHEST)
        + near_factor[..., None] * near
        + self_factor[..., None] * new_values.astype(f32)[:, None, :]
    )
    heads = (weighted / weight_sum[..., None]).astype(bf16).reshape(8, 512)

    summed = pl.pallas_call(
        output_kernel,
        out_shape=jax.ShapeDtypeStruct((2, 32, 64), f32),
        in_specs=[vmem()] * 2,
        out_specs=vmem(),
        scratch_shapes=[
            pltpu.VMEM((8, 8, 512), bf16),
            pltpu.VMEM((16, 32, 64), bf16),
            pltpu.VMEM((16, 32, 64), bf16),
            dma(8), dma(8), dma(16), dma(16), dma(1),
        ],
        compiler_params=params(3),
    )(heads, out_cols)
    return (
        summed.reshape(2, 4, 8, 64).transpose(1, 0, 2, 3).reshape(64, 64).astype(bf16)
    )


def solution(mesh):
    return jax.shard_map(
        shards,
        mesh=mesh,
        in_specs=(
            P(None, "req"),
            P("req", "head", None),
            P("head", "req"),
            P("req", "head", None, None),
            P("req"),
            P("req", None),
            P("req"),
        ),
        out_specs=P("head", "req"),
        check_vma=False,
    )
```

time: 292 us -> 114 us (0.39); the launches traced: 286 us -> 113 us
  waiting for transfers between devices: 185 us -> 0 us
  Pallas kernels: 0 us -> 96.6 us
  blocking collectives: 54.3 us -> 0 us
  between operations: 13.5 us -> 0.13 us
  starting transfers between devices: 11.7 us -> 0 us
  matrix products: 11.3 us -> 1.81 us
  other arithmetic: 3.76 us -> 9.77 us
    reduce_scatter x2 -> x0, waiting for transfers between devices: 185 us -> none  [the longest x1 150 us: shards(): lax.psum_scatter(jnp.dot(hidden, flat_weight, preferred_element_type=jnp....]
    pallas_call x0 -> x3, Pallas kernels: none -> 96.6 us  [the longest x1 43.2 us: shards(): pl.pallas_call(attend_kernel, out_shape=(jax.ShapeDtypeStruct((64, 8, 128...]
    all_gather x1 -> x0, blocking collectives: 54.3 us -> none  [shards(): lax.all_gather(output_per_head, 'req', axis=0, tiled=True)]
    all_to_all x1 -> x0, starting transfers between devices: 11.6 us -> none  [shards(): lax.all_to_all(outgoing, 'req', split_axis=0, concat_axis=0, tiled=True)]
    dot_general x7 -> x2, matrix products: 11.3 us -> 1.81 us  [the longest x1 1.56 us: shards(): jnp.einsum('rsq,sqd->rqd', factors, far, precision=lax.Precision.HIGHEST)]
    gather x2 -> x0, local copies, waits for them, and re-layouts: 5.63 us -> none  [the longest x1 4.97 us: shards(): outgoing = kv_pool[send_slots]]
  transfers between devices with their start and end apart: 3 -> 0, of which waited for: 2 -> 0; matrix products, arithmetic and copies ran while one was open for 2% -> 0% of each run, Pallas kernels for 0% -> 0%
where the time goes in v1:
time: 114 us; the launch traced here: 113 us
  Pallas kernels  96.6 us (85%)
  other arithmetic  9.77 us (9%)
  local copies, waits for them, and re-layouts  5.15 us (5%)
  matrix products  1.81 us (2%)
    pallas_call x1, Pallas kernels, shards(): pl.pallas_call(attend_kernel, out_shape=(jax.ShapeDtypeStruct((64, 8, 128...  43.2 us
    pallas_call x1, Pallas kernels, shards(): pl.pallas_call(output_kernel, out_shape=jax.ShapeDtypeStruct((2, 32, 64),...  28.7 us
    pallas_call x1, Pallas kernels, shards(): pl.pallas_call(project_kernel, out_shape=(jax.ShapeDtypeStruct((2, 8, 384...  24.7 us

profile of v1, /device:TPU:7, one launch (start us, length us, event | category | flops | bytes accessed | tf_op | source)
XLA Modules:
  0.0 113.4 jit_solution(4895246825175730653)
XLA Ops:
  0.0 0.9 reshape.205
  1.0 0.9 reshape.204
  1.9 0.9 pad_maximum_fusion
  2.8 24.7 %shard_map.73 = (f32[2,8,384]{2,1,0:T(8,128)}, bf16[8,64,512]{2,1,0:T(8,128)(2,1)}) custom-call(bf16[8,64,512]{2,1,0:T(8,128)(2,1)} %bitcast.69, bf16[64,512]{1,0:T(8,128)(2,1)} %bitcast.72), custom_call_target="tpu_custom_call" | custom-call | tf_op jit(solution)/shard_map/pallas_call | solution.py:326
  27.5 0.7 slice_bitcast_fusion
  28.2 0.7 convert_element_type.53
  28.8 0.1 subtract_convert_fusion.1
  29.0 0.9 subtract_convert_fusion
  29.8 0.7 subtract_clamp_fusion
  30.6 0.7 broadcast_compare_fusion
  31.3 0.8 select_reduce_fusion
  32.1 0.1 slice_compare_fusion
  32.2 0.2 fusion.11
  32.4 0.1 copy.32
  32.5 0.1 slice_reduce_fusion.2
  32.6 0.1 broadcast_in_dim.37
  32.7 0.7 pad_maximum_fusion.1.msg_ref
  33.5 0.7 fusion.20.q_ref
  34.1 0.6 broadcast_bitcast_fusion.valid_ref
  34.7 43.2 %shard_map.74 = (bf16[64,8,128]{2,1,0:T(8,128)(2,1)}, f32[32,128]{1,0:T(8,128)}, f32[32,128]{1,0:T(8,128)}, f32[32,128]{1,0:T(8,128)}) custom-call(s32[64]{0:T(128)} %slots_ref.1, bf16[64,8,128]{2,1,0:T(8,128)(2,1)} %pad_maximum_fusion.1.msg_ref, bf16[32,128]{1,0:T(8,128)(2,1)} %fusion.20.q_ref, s32[32,128]{1,0:T(8,128)} %broadcast_bitcast_fusion.valid_ref, ...), custom_call_target="tpu_custom_call" | custom-call | tf_op jit(solution)/shard_map/pallas_call | solution.py:365
  77.9 0.8 slice_reduce_fusion
  78.8 0.1 reshape_squeeze.6
  78.9 1.0 slice_convert_fusion
  79.9 0.4 slice_add_fusion.2
  80.3 0.1 copy.25
  80.4 0.1 select_reduce_fusion.1
  80.5 0.1 maximum_convert_fusion
  80.6 0.2 multiply_reduce_fusion.1
  80.8 0.1 copy.27
  80.9 0.2 multiply_reduce_fusion
  81.0 0.1 reshape_squeeze.7
  81.1 0.7 fusion.14
  81.8 1.6 %fusion.4.heads_ref = bf16[8,512]{1,0:T(8,128)(2,1)} fusion(bf16[64,4,128]{2,1,0:T(4,128)(2,1)S(1)} %get-tuple-element.23, f32[32,128]{1,0:T(8,128)} %get-tuple-element.14, f32[8,4]{0,1:T(4,128)S(1)} %get-tuple-element.17, f32[8,128]{1,0:T(8,128)S(1)} %fusion.14, f32[8,4]{0,1:T(4,128)S(1)} %get-tuple-element.19, f32[8,4]{0,1:T(4,128)S(1)} %get-tuple-element.18, ...), kind=kOutput, calls=%fused_computation.5 | convolution fusion | flops 3176448 | bytes 96256 | tf_op jit(solution)/shard_map/rsq,sqd->rqd/dot_general | solution.py:406
  83.4 28.7 %shard_map.75 = f32[2,32,64]{2,1,0:T(8,128)} custom-call(bf16[8,512]{1,0:T(8,128)(2,1)} %fusion.4.heads_ref, bf16[8,64,512]{2,1,0:T(8,128)(2,1)} %get-tuple-element.16.wg_ref), custom_call_target="tpu_custom_call" | custom-call | tf_op jit(solution)/shard_map/pallas_call | solution.py:412
  112.1 0.8 convert_bitcast_fusion
  112.8 0.6 copy.28
  (9 shorter events, 0.1 us)

commit v2 on v0

v2 whole, which is shorter than its diff:
```python
import jax
import jax.numpy as jnp
from jax import lax
from jax.experimental import pallas as pl
from jax.experimental.pallas import tpu as pltpu
from jax.sharding import PartitionSpec as P

ROPE_BASE = 500000.0
NEG_FILL = -1e30
SCALE = 128 ** (-0.5)


def rope_angles(lengths, width):
    exponent = jnp.arange(width // 2, dtype=jnp.float32) * (2.0 / width)
    inverse = 1.0 / ROPE_BASE**exponent
    return lengths.astype(jnp.float32)[:, None] * inverse[None, :]


def remote(src, dst, send, recv, req, head=None):
    where = {"req": req} if head is None else {"req": req, "head": head}
    return pltpu.make_async_remote_copy(
        src_ref=src, dst_ref=dst, send_sem=send, recv_sem=recv,
        device_id=where, device_id_type=pl.DeviceIdType.MESH,
    )


def greet(barrier, req, head=None):
    where = {"req": req} if head is None else {"req": req, "head": head}
    pl.semaphore_signal(barrier, inc=1, device_id=where, device_id_type=pl.DeviceIdType.MESH)


def for_each(start, stop, body):
    def step(i, carry):
        body(i)
        return carry
    lax.fori_loop(start, stop, step, 0)


def place(req):
    return req // 16, lax.rem(req // 2, 8), lax.rem(req, 2)


def split_three(v):
    high = v.astype(jnp.bfloat16).astype(jnp.float32)
    rest = v - high
    mid = rest.astype(jnp.bfloat16).astype(jnp.float32)
    return high, mid, rest - mid


def dot_nt(a, b):
    return lax.dot_general(a, b, (((1,), (1,)), ((), ())), preferred_element_type=jnp.float32)


def dot_tn(a, b):
    return lax.dot_general(a, b, (((0,), (0,)), ((), ())), preferred_element_type=jnp.float32)


def layer_kernel(
    slots_ref, lengths_ref, table_ref, cos_ref, sin_ref, pay_ref, wo_ref, kv_ref, out_ref,
    gathered, wide, partial, parts, pages, ask_buf, asked, scores, reply, back, heads_buf, rows,
    piece, pieces, own, s1, r1, s2, r2, s3, r3, s4, r4, s5, r5, s6, r6, s7, r7,
):
    bf16, f32 = jnp.bfloat16, jnp.float32
    req = lax.axis_index("req")
    z = lax.axis_index("head")
    x, y, c = place(req)
    xc = x * 2 + c
    yc = y * 2 + c
    mine = (z // 2) == x
    spot = c * 8 + z

    def at_xc(i):
        return (i // 2) * 16 + y * 2 + lax.rem(i, 2)

    def dest(k):
        return (k // 4) * 16 + y * 2 + lax.rem(k // 2, 2), x * 2 + lax.rem(k, 2)

    def origin(k):
        return (z // 2) * 16 + y * 2 + k // 8, lax.rem(k, 8)

    def is_me(pair):
        return jnp.logical_and(pair[0] == req, pair[1] == z)

    barrier = pltpu.get_barrier_semaphore()
    for_each(1, 64, lambda k: greet(barrier, lax.rem(req + k, 64)))

    def hello(k):
        @pl.when(jnp.logical_not(is_me(origin(k))))
        def _():
            greet(barrier, *origin(k))

    for_each(0, 16, hello)
    load = pltpu.make_async_copy(kv_ref, pages, own.at[0])
    load.start()
    own_pay = pltpu.make_async_copy(pay_ref.at[xc], gathered.at[xc], own.at[1])
    own_wo = pltpu.make_async_copy(wo_ref, wide.at[xc], own.at[2])
    own_pay.start()
    own_wo.start()

    row = lax.broadcasted_iota(jnp.int32, (8, 128), 0)
    lane = lax.broadcasted_iota(jnp.int32, (8, 128), 1)
    long = jnp.zeros((8, 128), jnp.int32)
    for i in range(8):
        long = jnp.where(row == i, lengths_ref[i], long)
    table = table_ref[...]
    valid = jnp.zeros((8, 128), jnp.int32)
    for p in range(16):
        tokens = jnp.clip(long - p * 128, 0, 128)
        valid = valid + jnp.where(table[:, p : p + 1] == lane, tokens, 0)
    spread = (
        lax.broadcasted_iota(jnp.int32, (128, 512), 0) - 64
        == lax.broadcasted_iota(jnp.int32, (128, 512), 1) // 8
    )
    wanted = jnp.dot(
        valid.astype(f32).astype(bf16),
        jnp.where(spread, 1.0, 0.0).astype(bf16),
        preferred_element_type=f32,
    )
    part8 = lax.rem(lax.broadcasted_iota(jnp.int32, (8, 512), 1), 8)
    owned = [
        jnp.where(jnp.logical_and(wanted > 0.0, part8 == q), 1.0, 0.0) for q in range(4)
    ]
    asking = owned + [jnp.where(part8 >= 4, wanted, 0.0)]
    owned = jnp.concatenate(owned, axis=0)
    asking = jnp.concatenate(asking, axis=0)
    valid = jnp.concatenate([valid] * 4, axis=0)

    @pl.when(mine)
    def _():
        pl.semaphore_wait(barrier, 63 + 15)

    @pl.when(jnp.logical_not(mine))
    def _():
        pl.semaphore_wait(barrier, 63 + 16)

    def send_pay(k):
        peer = lax.rem(xc + k, 8)
        return remote(pay_ref.at[peer], gathered.at[xc], s1.at[k], r1.at[k], at_xc(peer))

    def send_part(k):
        peer = lax.rem(yc + k, 16)
        return remote(partial.at[peer], parts.at[yc], s2.at[k], r2.at[k], x * 16 + peer)

    def send_wo(k):
        peer = lax.rem(xc + k, 8)
        return remote(wo_ref, wide.at[xc], s3.at[k], r3.at[k], at_xc(peer))

    def ask(k):
        peer = lax.rem(req + k, 64)
        return remote(ask_buf.at[peer], asked.at[req], s4.at[k], r4.at[k], peer)

    def answer(k):
        peer = lax.rem(req - k + 64, 64)
        return remote(reply.at[peer], back.at[req], s5.at[k], r5.at[k], peer)

    def send_rows(k):
        peer = x * 16 + lax.rem(y + k, 8) * 2 + c
        return remote(heads_buf, rows.at[y], s6.at[k], r6.at[k], peer)

    def push(k):
        return remote(piece.at[k], pieces.at[spot], s7.at[k], r7.at[spot], *dest(k))

    for_each(1, 8, lambda k: send_pay(k).start())
    own_pay.wait()
    for_each(1, 8, lambda k: send_pay(k).wait_recv())
    for_each(1, 8, lambda k: send_wo(k).start())
    sums = dot_tn(
        gathered[:, :, :128].reshape(512, 128), gathered[:, :, 128:].reshape(512, 384)
    )
    partial[...] = sums.reshape(16, 8, 384)
    own_part = pltpu.make_async_copy(partial.at[yc], parts.at[yc], own.at[1])
    own_part.start()
    for_each(1, 16, lambda k: send_part(k).start())
    own_part.wait()
    for_each(1, 16, lambda k: send_part(k).wait_recv())
    total = parts[0:2]
    for i in range(1, 8):
        total = total + parts[2 * i : 2 * i + 2]
    made = [total[h // 3, :, 128 * (h % 3) : 128 * (h % 3) + 128] for h in range(6)]
    cosine, sine = cos_ref[...], sin_ref[...]

    def turn(v):
        return (v * cosine + pltpu.roll(v, 64, 1) * sine).astype(bf16).astype(f32)

    queries = jnp.concatenate([turn(made[q]) for q in range(4)], axis=0)
    new_keys = jnp.concatenate([turn(made[4])] * 4, axis=0)
    new_values = jnp.concatenate([made[5].astype(bf16).astype(f32)] * 4, axis=0)
    self_scores = jnp.sum(queries * new_keys, axis=1, keepdims=True) * SCALE
    ask_rows = dot_tn(
        asking.astype(bf16),
        jnp.concatenate([queries, jnp.ones((8, 128), f32)], axis=0).astype(bf16),
    )
    ask_buf[...] = ask_rows.reshape(64, 8, 128).astype(bf16)
    own_ask = pltpu.make_async_copy(ask_buf.at[req], asked.at[req], own.at[1])
    own_ask.start()
    for_each(1, 64, lambda k: ask(k).start())
    load.wait()

    lane32 = lax.broadcasted_iota(jnp.int32, (32, 128), 1)
    queries = queries.astype(bf16)

    def score(e, top):
        s = dot_nt(queries, pages[e, :, 0:128]) * SCALE
        tokens = jnp.sum(jnp.where(lane32 == e, valid, 0), axis=1, keepdims=True)
        s = jnp.where(lane32 < tokens, s, NEG_FILL)
        scores[e] = s
        return jnp.maximum(top, s)

    near_max = lax.fori_loop(0, 64, score, jnp.full((32, 128), NEG_FILL, f32), unroll=8)
    near_max = jnp.max(near_max, axis=1, keepdims=True)

    def gather(e, carry):
        acc, weight = carry
        s = scores[e]
        w = jnp.where(s > 0.5 * NEG_FILL, jnp.exp(s - near_max), 0.0)
        return acc + jnp.dot(w.astype(bf16), pages[e, :, 128:256], preferred_element_type=f32), weight + w

    zero = jnp.zeros((32, 128), f32)
    near, near_sum = lax.fori_loop(0, 64, gather, (zero, zero), unroll=8)
    near_sum = jnp.sum(near_sum, axis=1, keepdims=True)

    own_ask.wait()
    batch = 16
    row3 = lax.broadcasted_iota(jnp.int32, (batch, 8, 128), 1)
    lane3 = lax.broadcasted_iota(jnp.int32, (batch, 8, 128), 2)
    own_answer = pltpu.make_async_copy(reply.at[req], back.at[req], own.at[0])

    def serve(j, carry):
        first = j * batch

        def heard(k):
            @pl.when(k > 0)
            def _():
                ask(k).wait_recv()

        def tell(k):
            @pl.when(k > 0)
            def _():
                answer(k).start()

        for_each(first, first + batch, heard)
        sources = [lax.rem(req - first - i + 64, 64) for i in range(batch)]
        slots = [slots_ref[g] for g in sources]
        query, limit = [], []
        for g in sources:
            both = asked[g].astype(f32)
            other = pltpu.roll(both, 4, 0)
            query.append(jnp.where(row < 4, both, other).astype(bf16))
            limit.append(jnp.where(row < 4, other, both))
        limit = jnp.stack(limit)
        s = jnp.stack([dot_nt(query[i], pages[slots[i], :, 0:128]) for i in range(batch)]) * SCALE
        mask = lane3.astype(f32) < limit
        s = jnp.where(mask, s, NEG_FILL)
        m = jnp.max(s, axis=2, keepdims=True)
        w = jnp.where(mask, jnp.exp(s - m), 0.0)
        l = jnp.sum(w, axis=2, keepdims=True)
        m0, m1, m2 = split_three(jnp.broadcast_to(m, s.shape))
        l0, l1, l2 = split_three(jnp.broadcast_to(l, s.shape))
        stats = jnp.where(lane3 < 16, m0, jnp.where(lane3 < 32, m1, jnp.where(lane3 < 48, m2,
                jnp.where(lane3 < 64, l0, jnp.where(lane3 < 80, l1, l2)))))
        for i in range(batch):
            a = jnp.dot(
                w[i].astype(bf16), pages[slots[i], :, 128:256], preferred_element_type=f32
            )
            reply[sources[i]] = jnp.where(row < 4, a, stats[i]).astype(bf16)
        for_each(first, first + batch, tell)
        return carry

    lax.fori_loop(0, 64 // batch, serve, 0)
    own_answer.start()
    own_answer.wait()
    for_each(1, 64, lambda k: answer(k).wait_recv())

    far = back[...].astype(f32).reshape(512, 128).astype(bf16)
    pick_max = jnp.logical_and(lane < 48, lax.rem(lane, 16) == 0)
    pick_sum = jnp.logical_and(
        jnp.logical_and(lane >= 48, lane < 96), lax.rem(lane, 16) == 0
    )
    far_max = dot_nt(jnp.where(pick_max, 1.0, 0.0).astype(bf16), far)
    far_sum = dot_nt(jnp.where(pick_sum, 1.0, 0.0).astype(bf16), far)
    far_max = jnp.concatenate([pltpu.roll(far_max, 508, 1)] * 4, axis=0)
    far_sum = jnp.concatenate([pltpu.roll(far_sum, 508, 1)] * 4, axis=0)
    picked = owned > 0.5
    peak = jnp.max(jnp.where(picked, far_max, NEG_FILL), axis=1, keepdims=True)
    peak = jnp.maximum(jnp.maximum(peak, near_max), self_scores)
    factors = jnp.where(picked, jnp.exp(jnp.minimum(far_max - peak, 0.0)), 0.0)
    near_factor = jnp.exp(near_max - peak)
    self_factor = jnp.exp(self_scores - peak)
    weight_sum = (
        jnp.sum(jnp.where(picked, factors * far_sum, 0.0), axis=1, keepdims=True)
        + near_factor * near_sum + self_factor
    )
    high = factors.astype(bf16)
    low = (factors - high.astype(f32)).astype(bf16)
    weighted = (
        jnp.dot(high, far, preferred_element_type=f32)
        + jnp.dot(low, far, preferred_element_type=f32)
        + near_factor * near + self_factor * new_values
    )
    heads_buf[...] = (weighted / weight_sum).astype(bf16)

    own_rows = pltpu.make_async_copy(heads_buf, rows.at[y], own.at[0])
    own_rows.start()
    for_each(1, 8, lambda k: send_rows(k).start())
    own_wo.wait()
    for_each(1, 8, lambda k: send_wo(k).wait_recv())
    own_rows.wait()
    for_each(1, 8, lambda k: send_rows(k).wait_recv())
    heads = rows[...].astype(f32)
    heads = jnp.concatenate(
        [heads[:, 8 * q : 8 * q + 8].reshape(64, 128) for q in range(4)], axis=1
    ).astype(bf16)
    for i in range(8):
        tile = dot_nt(heads, wide[i]).astype(bf16)
        piece[2 * i] = tile[0:32]
        piece[2 * i + 1] = tile[32:64]

    def send(k):
        @pl.when(is_me(dest(k)))
        def _():
            pltpu.make_async_copy(piece.at[k], pieces.at[spot], r7.at[spot]).start()

        @pl.when(jnp.logical_not(is_me(dest(k))))
        def _():
            push(k).start()

    for_each(0, 16, send)
    for_each(1, 64, lambda k: ask(k).wait_send())
    for_each(1, 64, lambda k: answer(k).wait_send())
    for_each(1, 8, lambda k: send_pay(k).wait_send())
    for_each(1, 16, lambda k: send_part(k).wait_send())
    for_each(1, 8, lambda k: send_wo(k).wait_send())
    for_each(1, 8, lambda k: send_rows(k).wait_send())

    def receive(k):
        pltpu.make_async_copy(pieces.at[k], pieces.at[k], r7.at[k]).wait()

    for_each(0, 16, receive)
    totals = []
    for j in range(2):
        total = pieces[8 * j].astype(f32)
        for h in range(1, 8):
            total = total + pieces[8 * j + h].astype(f32)
        totals.append(total)
    out_ref[...] = jnp.concatenate(
        [totals[j][8 * i : 8 * i + 8] for i in range(4) for j in range(2)], axis=0
    ).astype(bf16)

    def sent(k):
        @pl.when(jnp.logical_not(is_me(dest(k))))
        def _():
            push(k).wait_send()

    for_each(0, 16, sent)


def vmem():
    return pl.BlockSpec(memory_space=pltpu.VMEM)


def params(ident):
    return pltpu.CompilerParams(collective_id=ident, has_side_effects=True)


def dma(count):
    return pltpu.SemaphoreType.DMA((count,))


def shards(hidden, query_key_value_weight, output_weight, kv_pool, lengths, page_table, send_slots):
    bf16, f32 = jnp.bfloat16, jnp.float32
    hidden_t = hidden.T.reshape(64, 4, 128).transpose(1, 0, 2)
    weight = query_key_value_weight.reshape(64, 2, 384).transpose(1, 0, 2)
    payload = jnp.concatenate(
        [
            jnp.broadcast_to(hidden_t[:, None], (4, 2, 64, 128)),
            jnp.broadcast_to(weight[None], (4, 2, 64, 384)),
        ],
        axis=-1,
    ).reshape(8, 64, 512)
    angles = rope_angles(lengths, 128)
    angles = jnp.concatenate([angles, angles], axis=1)
    sign = jnp.where(jnp.arange(128) < 64, -1.0, 1.0).astype(f32)
    smem = pl.BlockSpec(memory_space=pltpu.SMEM)
    return pl.pallas_call(
        layer_kernel,
        out_shape=jax.ShapeDtypeStruct((64, 64), bf16),
        in_specs=[smem, smem] + [vmem()] * 5 + [pl.BlockSpec(memory_space=pl.ANY)],
        out_specs=vmem(),
        scratch_shapes=[
            pltpu.VMEM((8, 64, 512), bf16),
            pltpu.VMEM((8, 64, 512), bf16),
            pltpu.VMEM((16, 8, 384), f32),
            pltpu.VMEM((16, 8, 384), f32),
            pltpu.VMEM((64, 128, 256), bf16),
            pltpu.VMEM((64, 8, 128), bf16),
            pltpu.VMEM((64, 8, 128), bf16),
            pltpu.VMEM((64, 32, 128), f32),
            pltpu.VMEM((64, 8, 128), bf16),
            pltpu.VMEM((64, 8, 128), bf16),
            pltpu.VMEM((32, 128), bf16),
            pltpu.VMEM((8, 32, 128), bf16),
            pltpu.VMEM((16, 32, 64), bf16),
            pltpu.VMEM((16, 32, 64), bf16),
            dma(3), dma(8), dma(8), dma(16), dma(16), dma(8), dma(8), dma(64), dma(64),
            dma(64), dma(64), dma(8), dma(8), dma(16), dma(16),
        ],
        compiler_params=params(1),
    )(
        send_slots, lengths, page_table, jnp.cos(angles), jnp.sin(angles) * sign,
        payload, output_weight.T, kv_pool.reshape(64, 128, 256),
    )


def solution(mesh):
    return jax.shard_map(
        shards,
        mesh=mesh,
        in_specs=(
            P(None, "req"),
            P("req", "head", None),
            P("head", "req"),
            P("req", "head", None, None),
            P("req"),
            P("req", None),
            P("req"),
        ),
        out_specs=P("head", "req"),
        check_vma=False,
    )
```

time: 292 us -> 72.9 us (0.25); the launches traced: 286 us -> 72.7 us
  waiting for transfers between devices: 185 us -> 0 us
  Pallas kernels: 0 us -> 67.1 us
  blocking collectives: 54.3 us -> 0 us
  between operations: 13.5 us -> 0.05 us
  starting transfers between devices: 11.7 us -> 0 us
  matrix products: 11.3 us -> 0 us
  local copies, waits for them, and re-layouts: 6.47 us -> 3.19 us
    reduce_scatter x2 -> x0, waiting for transfers between devices: 185 us -> none  [the longest x1 150 us: shards(): lax.psum_scatter(jnp.dot(hidden, flat_weight, preferred_element_type=jnp....]
    pallas_call x0 -> x1, Pallas kernels: none -> 67.1 us  [shards(): pl.pallas_call(layer_kernel, out_shape=jax.ShapeDtypeStruct((64, 64), bf1...]
    all_gather x1 -> x0, blocking collectives: 54.3 us -> none  [shards(): lax.all_gather(output_per_head, 'req', axis=0, tiled=True)]
    all_to_all x1 -> x0, starting transfers between devices: 11.6 us -> none  [shards(): lax.all_to_all(outgoing, 'req', split_axis=0, concat_axis=0, tiled=True)]
    dot_general x7 -> x0, matrix products: 11.3 us -> none  [the longest x1 4.58 us: page_stats(): jnp.einsum('nhqd,nhtd->nhqt', queries, pages[..., :head_dim], preferred_e...]
    gather x2 -> x0, local copies, waits for them, and re-layouts: 5.63 us -> none  [the longest x1 4.97 us: shards(): outgoing = kv_pool[send_slots]]
  transfers between devices with their start and end apart: 3 -> 0, of which waited for: 2 -> 0; matrix products, arithmetic and copies ran while one was open for 2% -> 0% of each run, Pallas kernels for 0% -> 0%
where the time goes in v2:
time: 72.9 us; the launch traced here: 72.7 us
  Pallas kernels  67.1 us (92%)
  local copies, waits for them, and re-layouts  3.19 us (4%)
  other arithmetic  2.3 us (3%)
    pallas_call x1, Pallas kernels, shards(): pl.pallas_call(layer_kernel, out_shape=jax.ShapeDtypeStruct((64, 64), bf1...  67.1 us

profile of v2, /device:TPU:7, one launch (start us, length us, event | category | flops | bytes accessed | tf_op | source)
XLA Modules:
  0.0 72.7 jit_solution(1499098917901836048)
XLA Ops:
  0.0 0.7 convert_element_type.3
  0.7 0.1 broadcast_multiply_fusion
  0.7 0.7 sine_multiply_fusion
  1.5 0.9 %reshape.26 = bf16[64,4,128]{2,1,0:T(4,128)(2,1)S(1)} reshape(bf16[64,512]{1,0:T(8,128)(2,1)} %bitcast.13) | data formatting | bytes 131072 | tf_op jit(solution)/shard_map/reshape | solution.py:371
  2.4 0.9 %reshape.27 = bf16[64,2,384]{2,1,0:T(2,128)(2,1)S(1)} reshape(bf16[64,1,768]{2,0,1:T(8,128)(2,1)} %param.8) | data formatting | bytes 196608 | tf_op jit(solution)/shard_map/reshape | solution.py:372
  3.4 0.8 %pad_maximum_fusion = bf16[4,2,64,512]{3,2,1,0:T(8,128)(2,1)} fusion(bf16[4,2,64,384]{3,2,1,0:T(8,128)(2,1)S(1)} %broadcast_in_dim.26, bf16[4,2,64,128]{3,2,1,0:T(8,128)(2,1)S(1)} %broadcast_in_dim.14), kind=kLoop, calls=%fused_computation | loop fusion | flops 1048576 | bytes 1048576 | tf_op jit(solution)/shard_map/concatenate | solution.py:373
  4.2 67.1 %shard_map.73 = bf16[64,64]{1,0:T(8,128)(2,1)} custom-call(s32[64]{0:T(128)} %slots_ref.1, s32[8]{0:T(128)} %lengths_ref.1, s32[8,16]{1,0:T(8,128)} %table_ref.1, f32[8,128]{1,0:T(8,128)} %get-tuple-element.6.cos_ref, f32[8,128]{1,0:T(8,128)} %get-tuple-element.5.sin_ref, bf16[8,64,512]{2,1,0:T(8,128)(2,1)} %bitcast.9, bf16[64,512]{1,0:T(8,128)(2,1)} %bitcast.12, ...), custom_call_target="tpu_custom_call" | custom-call | tf_op jit(solution)/shard_map/pallas_call | solution.py:384
  71.3 1.3 %copy.11 = bf16[64,64]{1,0:T(8,128)(2,1)} copy(bf16[64,64]{1,0:T(8,128)(2,1)} %shard_map.73) | data formatting | bytes 16384
  (6 shorter events, 0.1 us)

commit v3 on v2

--- a/solution.py
+++ b/solution.py
@@ -1,5 +1,6 @@
 import jax
 import jax.numpy as jnp
+import numpy as np
 from jax import lax
 from jax.experimental import pallas as pl
 from jax.experimental.pallas import tpu as pltpu
@@ -8,12 +9,6 @@
 ROPE_BASE = 500000.0
 NEG_FILL = -1e30
 SCALE = 128 ** (-0.5)
-
-
-def rope_angles(lengths, width):
-    exponent = jnp.arange(width // 2, dtype=jnp.float32) * (2.0 / width)
-    inverse = 1.0 / ROPE_BASE**exponent
-    return lengths.astype(jnp.float32)[:, None] * inverse[None, :]
 
 
 def remote(src, dst, send, recv, req, head=None):
@@ -56,9 +51,10 @@
 
 
 def layer_kernel(
-    slots_ref, lengths_ref, table_ref, cos_ref, sin_ref, pay_ref, wo_ref, kv_ref, out_ref,
-    gathered, wide, partial, parts, pages, ask_buf, asked, scores, reply, back, heads_buf, rows,
+    slots_ref, lengths_ref, table_ref, base_ref, hid_ref, w_ref, wo_ref, kv_ref, out_ref,
+    gathered, weights, wide, partial, parts, pages, limits, ask_buf, asked, scores, reply, back, heads_buf, rows,
     piece, pieces, own, s1, r1, s2, r2, s3, r3, s4, r4, s5, r5, s6, r6, s7, r7,
+    s8, r8,
 ):
     bf16, f32 = jnp.bfloat16, jnp.float32
     req = lax.axis_index("req")
@@ -81,6 +77,9 @@
     def is_me(pair):
         return jnp.logical_and(pair[0] == req, pair[1] == z)
 
+    def block(i, width):
+        return pl.ds(pl.multiple_of(i * width, width), width)
+
     barrier = pltpu.get_barrier_semaphore()
     for_each(1, 64, lambda k: greet(barrier, lax.rem(req + k, 64)))
 
@@ -92,10 +91,80 @@
     for_each(0, 16, hello)
     load = pltpu.make_async_copy(kv_ref, pages, own.at[0])
     load.start()
-    own_pay = pltpu.make_async_copy(pay_ref.at[xc], gathered.at[xc], own.at[1])
+    own_pay = pltpu.make_async_copy(hid_ref.at[:, block(x, 128)], gathered.at[xc], own.at[1])
+    own_w = pltpu.make_async_copy(w_ref.at[:, block(c, 384)], weights.at[xc], own.at[3])
     own_wo = pltpu.make_async_copy(wo_ref, wide.at[xc], own.at[2])
     own_pay.start()
+    own_w.start()
     own_wo.start()
+
+    @pl.when(mine)
+    def _():
+        pl.semaphore_wait(barrier, 63 + 15)
+
+    @pl.when(jnp.logical_not(mine))
+    def _():
+        pl.semaphore_wait(barrier, 63 + 16)
+
+    def send_pay(k):
+        peer = lax.rem(xc + k, 8)
+        return remote(
+            hid_ref.at[:, block(peer // 2, 128)], gathered.at[xc], s1.at[k], r1.at[k], at_xc(peer)
+        )
+
+    def send_w(k):
+        far = lax.rem(x + 1 + 2 * (k // 2), 4) * 2 + lax.rem(k, 2)
+        return remote(
+            w_ref.at[:, block(lax.rem(k, 2), 384)], weights.at[xc], s8.at[k], r8.at[xc], at_xc(far)
+        )
+
+    def near_w():
+        return remote(
+            w_ref.at[:, block(1 - c, 384)], weights.at[xc], s8.at[4], r8.at[xc],
+            at_xc(x * 2 + 1 - c),
+        )
+
+    def pass_w(k):
+        source = lax.rem(x + 3 + 2 * k, 4) * 2 + k
+        target = lax.rem(x + 1 + 2 * k, 4) * 2 + c
+        return remote(
+            weights.at[source], weights.at[source], s8.at[5 + k], r8.at[source], at_xc(target)
+        )
+
+    def have_w(source):
+        remote(
+            weights.at[source], weights.at[source], s8.at[0], r8.at[source], at_xc(source)
+        ).wait_recv()
+
+    def send_part(k):
+        peer = lax.rem(yc + k, 16)
+        return remote(partial.at[peer], parts.at[yc], s2.at[k], r2.at[k], x * 16 + peer)
+
+    def send_wo(k):
+        peer = lax.rem(xc + k, 8)
+        return remote(wo_ref, wide.at[xc], s3.at[k], r3.at[k], at_xc(peer))
+
+    def ask(k):
+        peer = lax.rem(req + k, 64)
+        return remote(ask_buf.at[peer], asked.at[req], s4.at[k], r4.at[k], peer)
+
+    def answer(k):
+        peer = lax.rem(req - k + 64, 64)
+        return remote(reply.at[peer], back.at[req], s5.at[k], r5.at[k], peer)
+
+    def send_rows(k):
+        peer = x * 16 + lax.rem(y + k, 8) * 2 + c
+        return remote(heads_buf, rows.at[y], s6.at[k], r6.at[k], peer)
+
+    def push(k):
+        return remote(piece.at[k], pieces.at[spot], s7.at[k], r7.at[spot], *dest(k))
+
+    for_each(0, 4, lambda k: send_w(k).start())
+    for_each(1, 8, lambda k: send_pay(k).start())
+    near_w().start()
+    for k in range(2):
+        have_w(lax.rem(x + 3 + 2 * k, 4) * 2 + k)
+        pass_w(k).start()
 
     row = lax.broadcasted_iota(jnp.int32, (8, 128), 0)
     lane = lax.broadcasted_iota(jnp.int32, (8, 128), 1)
@@ -125,59 +194,37 @@
     asking = jnp.concatenate(asking, axis=0)
     valid = jnp.concatenate([valid] * 4, axis=0)
 
-    @pl.when(mine)
-    def _():
-        pl.semaphore_wait(barrier, 63 + 15)
-
-    @pl.when(jnp.logical_not(mine))
-    def _():
-        pl.semaphore_wait(barrier, 63 + 16)
-
-    def send_pay(k):
-        peer = lax.rem(xc + k, 8)
-        return remote(pay_ref.at[peer], gathered.at[xc], s1.at[k], r1.at[k], at_xc(peer))
-
-    def send_part(k):
-        peer = lax.rem(yc + k, 16)
-        return remote(partial.at[peer], parts.at[yc], s2.at[k], r2.at[k], x * 16 + peer)
-
-    def send_wo(k):
-        peer = lax.rem(xc + k, 8)
-        return remote(wo_ref, wide.at[xc], s3.at[k], r3.at[k], at_xc(peer))
-
-    def ask(k):
-        peer = lax.rem(req + k, 64)
-        return remote(ask_buf.at[peer], asked.at[req], s4.at[k], r4.at[k], peer)
-
-    def answer(k):
-        peer = lax.rem(req - k + 64, 64)
-        return remote(reply.at[peer], back.at[req], s5.at[k], r5.at[k], peer)
-
-    def send_rows(k):
-        peer = x * 16 + lax.rem(y + k, 8) * 2 + c
-        return remote(heads_buf, rows.at[y], s6.at[k], r6.at[k], peer)
-
-    def push(k):
-        return remote(piece.at[k], pieces.at[spot], s7.at[k], r7.at[spot], *dest(k))
-
-    for_each(1, 8, lambda k: send_pay(k).start())
+    lane32 = lax.broadcasted_iota(jnp.int32, (32, 128), 1)
+
+    def limit_page(e, carry):
+        tokens = jnp.sum(jnp.where(lane32 == e, valid, 0), axis=1, keepdims=True)
+        limits[e] = jnp.where(lane32 < tokens, 0.0, NEG_FILL)
+        return carry
+
+    lax.fori_loop(0, 64, limit_page, 0, unroll=8)
+    angles = long.astype(f32) * base_ref[...]
+    cosine = jnp.cos(angles)
+    sine = jnp.where(lane < 64, -jnp.sin(angles), jnp.sin(angles))
+
     own_pay.wait()
+    own_w.wait()
     for_each(1, 8, lambda k: send_pay(k).wait_recv())
+    for k in range(2):
+        have_w(lax.rem(x + 3 + 2 * k, 4) * 2 + 1 - k)
+        have_w(lax.rem(x + 2, 4) * 2 + k)
+    have_w(x * 2 + 1 - c)
     for_each(1, 8, lambda k: send_wo(k).start())
-    sums = dot_tn(
-        gathered[:, :, :128].reshape(512, 128), gathered[:, :, 128:].reshape(512, 384)
-    )
-    partial[...] = sums.reshape(16, 8, 384)
+    sums = dot_tn(gathered[...].reshape(512, 128), weights[...].reshape(512, 384))
+    partial[...] = sums.reshape(16, 8, 384).astype(bf16)
     own_part = pltpu.make_async_copy(partial.at[yc], parts.at[yc], own.at[1])
     own_part.start()
     for_each(1, 16, lambda k: send_part(k).start())
     own_part.wait()
     for_each(1, 16, lambda k: send_part(k).wait_recv())
-    total = parts[0:2]
+    total = parts[0:2].astype(f32)
     for i in range(1, 8):
-        total = total + parts[2 * i : 2 * i + 2]
+        total = total + parts[2 * i : 2 * i + 2].astype(f32)
     made = [total[h // 3, :, 128 * (h % 3) : 128 * (h % 3) + 128] for h in range(6)]
-    cosine, sine = cos_ref[...], sin_ref[...]
 
     def turn(v):
         return (v * cosine + pltpu.roll(v, 64, 1) * sine).astype(bf16).astype(f32)
@@ -196,13 +243,11 @@
     for_each(1, 64, lambda k: ask(k).start())
     load.wait()
 
-    lane32 = lax.broadcasted_iota(jnp.int32, (32, 128), 1)
     queries = queries.astype(bf16)
 
     def score(e, top):
         s = dot_nt(queries, pages[e, :, 0:128]) * SCALE
-        tokens = jnp.sum(jnp.where(lane32 == e, valid, 0), axis=1, keepdims=True)
-        s = jnp.where(lane32 < tokens, s, NEG_FILL)
+        s = jnp.where(limits[e] == 0.0, s, NEG_FILL)
         scores[e] = s
         return jnp.maximum(top, s)
 
@@ -328,6 +373,10 @@
     for_each(1, 64, lambda k: ask(k).wait_send())
     for_each(1, 64, lambda k: answer(k).wait_send())
     for_each(1, 8, lambda k: send_pay(k).wait_send())
+    for_each(0, 4, lambda k: send_w(k).wait_send())
+    near_w().wait_send()
+    for k in range(2):
+        pass_w(k).wait_send()
     for_each(1, 16, lambda k: send_part(k).wait_send())
     for_each(1, 8, lambda k: send_wo(k).wait_send())
     for_each(1, 8, lambda k: send_rows(k).wait_send())
@@ -368,18 +417,8 @@
 
 def shards(hidden, query_key_value_weight, output_weight, kv_pool, lengths, page_table, send_slots):
     bf16, f32 = jnp.bfloat16, jnp.float32
-    hidden_t = hidden.T.reshape(64, 4, 128).transpose(1, 0, 2)
-    weight = query_key_value_weight.reshape(64, 2, 384).transpose(1, 0, 2)
-    payload = jnp.concatenate(
-        [
-            jnp.broadcast_to(hidden_t[:, None], (4, 2, 64, 128)),
-            jnp.broadcast_to(weight[None], (4, 2, 64, 384)),
-        ],
-        axis=-1,
-    ).reshape(8, 64, 512)
-    angles = rope_angles(lengths, 128)
-    angles = jnp.concatenate([angles, angles], axis=1)
-    sign = jnp.where(jnp.arange(128) < 64, -1.0, 1.0).astype(f32)
+    exponent = np.arange(128) % 64 * (2.0 / 128)
+    base = np.broadcast_to(ROPE_BASE ** -exponent, (8, 128)).astype(np.float32)
     smem = pl.BlockSpec(memory_space=pltpu.SMEM)
     return pl.pallas_call(
         layer_kernel,
@@ -387,11 +426,13 @@
         in_specs=[smem, smem] + [vmem()] * 5 + [pl.BlockSpec(memory_space=pl.ANY)],
         out_specs=vmem(),
         scratch_shapes=[
+            pltpu.VMEM((8, 64, 128), bf16),
+            pltpu.VMEM((8, 64, 384), bf16),
             pltpu.VMEM((8, 64, 512), bf16),
-            pltpu.VMEM((8, 64, 512), bf16),
-            pltpu.VMEM((16, 8, 384), f32),
-            pltpu.VMEM((16, 8, 384), f32),
+            pltpu.VMEM((16, 8, 384), bf16),
+            pltpu.VMEM((16, 8, 384), bf16),
             pltpu.VMEM((64, 128, 256), bf16),
+            pltpu.VMEM((64, 32, 128), f32),
             pltpu.VMEM((64, 8, 128), bf16),
             pltpu.VMEM((64, 8, 128), bf16),
             pltpu.VMEM((64, 32, 128), f32),
@@ -401,13 +442,14 @@
             pltpu.VMEM((8, 32, 128), bf16),
             pltpu.VMEM((16, 32, 64), bf16),
             pltpu.VMEM((16, 32, 64), bf16),
-            dma(3), dma(8), dma(8), dma(16), dma(16), dma(8), dma(8), dma(64), dma(64),
+            dma(4), dma(8), dma(8), dma(16), dma(16), dma(8), dma(8), dma(64), dma(64),
             dma(64), dma(64), dma(8), dma(8), dma(16), dma(16),
+            dma(7), dma(8),
         ],
         compiler_params=params(1),
     )(
-        send_slots, lengths, page_table, jnp.cos(angles), jnp.sin(angles) * sign,
-        payload, output_weight.T, kv_pool.reshape(64, 128, 256),
+        send_slots, lengths, page_table, jnp.asarray(base),
+        hidden.T, query_key_value_weight.reshape(64, 768), output_weight.T, kv_pool.reshape(64, 128, 256),
     )
 
 

time: 72.9 us -> 67.3 us (0.923)
  other arithmetic: 2.3 us -> 0 us
  local copies, waits for them, and re-layouts: 3.19 us -> 1.32 us
  Pallas kernels: 67.1 us -> 65.8 us
    reshape x2 -> x0, local copies, waits for them, and re-layouts: 1.78 us -> none  [the longest x1 0.92 us: shards(): weight = query_key_value_weight.reshape(64, 2, 384).transpose(1, 0, 2)]
    pallas_call x1, Pallas kernels: 67.1 us -> 65.8 us  [shards(): pl.pallas_call(layer_kernel, out_shape=jax.ShapeDtypeStruct((64, 64), bf1...]
    concatenate x1 -> x0, other arithmetic: 0.84 us -> none  [shards(): jnp.concatenate([jnp.broadcast_to(hidden_t[:, None], (4, 2, 64, 128)), jn...]
    mul x2 -> x0, other arithmetic: 0.79 us -> none  [the longest x1 0.72 us: shards(): jnp.sin(angles) * sign]
where the time goes in v3:
time: 67.3 us; the launch traced here: 67.1 us
  Pallas kernels  65.8 us (98%)
  local copies, waits for them, and re-layouts  1.32 us (2%)
    pallas_call x1, Pallas kernels, shards(): pl.pallas_call(layer_kernel, out_shape=jax.ShapeDtypeStruct((64, 64), bf1...  65.8 us

profile of v3, /device:TPU:7, one launch (start us, length us, event | category | flops | bytes accessed | tf_op | source)
XLA Modules:
  0.0 67.1 jit_solution(7424758358145173128)
XLA Ops:
  0.0 65.8 %shard_map.82 = bf16[64,64]{1,0:T(8,128)(2,1)} custom-call(s32[64]{0:T(128)} %slots_ref.1, s32[8]{0:T(128)} %lengths_ref.1, s32[8,16]{1,0:T(8,128)} %table_ref.1, f32[8,128]{1,0:T(8,128)} %constant.2.clone.base_ref, bf16[64,512]{1,0:T(8,128)(2,1)} %bitcast.6, bf16[64,768]{1,0:T(8,128)(2,1)} %bitcast.5, bf16[64,512]{1,0:T(8,128)(2,1)} %bitcast.7, ...), custom_call_target="tpu_custom_call" | custom-call | tf_op jit(solution)/shard_map/pallas_call | solution.py:423
  65.8 1.3 %copy.10 = bf16[64,64]{1,0:T(8,128)(2,1)} copy(bf16[64,64]{1,0:T(8,128)(2,1)} %shard_map.82) | data formatting | bytes 16384

commit v4 on v3

--- a/solution.py
+++ b/solution.py
@@ -194,14 +194,6 @@
     asking = jnp.concatenate(asking, axis=0)
     valid = jnp.concatenate([valid] * 4, axis=0)
 
-    lane32 = lax.broadcasted_iota(jnp.int32, (32, 128), 1)
-
-    def limit_page(e, carry):
-        tokens = jnp.sum(jnp.where(lane32 == e, valid, 0), axis=1, keepdims=True)
-        limits[e] = jnp.where(lane32 < tokens, 0.0, NEG_FILL)
-        return carry
-
-    lax.fori_loop(0, 64, limit_page, 0, unroll=8)
     angles = long.astype(f32) * base_ref[...]
     cosine = jnp.cos(angles)
     sine = jnp.where(lane < 64, -jnp.sin(angles), jnp.sin(angles))
@@ -213,12 +205,19 @@
         have_w(lax.rem(x + 3 + 2 * k, 4) * 2 + 1 - k)
         have_w(lax.rem(x + 2, 4) * 2 + k)
     have_w(x * 2 + 1 - c)
-    for_each(1, 8, lambda k: send_wo(k).start())
     sums = dot_tn(gathered[...].reshape(512, 128), weights[...].reshape(512, 384))
     partial[...] = sums.reshape(16, 8, 384).astype(bf16)
     own_part = pltpu.make_async_copy(partial.at[yc], parts.at[yc], own.at[1])
     own_part.start()
     for_each(1, 16, lambda k: send_part(k).start())
+    lane32 = lax.broadcasted_iota(jnp.int32, (32, 128), 1)
+
+    def limit_page(e, carry):
+        tokens = jnp.sum(jnp.where(lane32 == e, valid, 0), axis=1, keepdims=True)
+        limits[e] = jnp.where(lane32 < tokens, 0.0, NEG_FILL)
+        return carry
+
+    lax.fori_loop(0, 64, limit_page, 0, unroll=8)
     own_part.wait()
     for_each(1, 16, lambda k: send_part(k).wait_recv())
     total = parts[0:2].astype(f32)
@@ -253,16 +252,6 @@
 
     near_max = lax.fori_loop(0, 64, score, jnp.full((32, 128), NEG_FILL, f32), unroll=8)
     near_max = jnp.max(near_max, axis=1, keepdims=True)
-
-    def gather(e, carry):
-        acc, weight = carry
-        s = scores[e]
-        w = jnp.where(s > 0.5 * NEG_FILL, jnp.exp(s - near_max), 0.0)
-        return acc + jnp.dot(w.astype(bf16), pages[e, :, 128:256], preferred_element_type=f32), weight + w
-
-    zero = jnp.zeros((32, 128), f32)
-    near, near_sum = lax.fori_loop(0, 64, gather, (zero, zero), unroll=8)
-    near_sum = jnp.sum(near_sum, axis=1, keepdims=True)
 
     own_ask.wait()
     batch = 16
@@ -313,6 +302,17 @@
 
     lax.fori_loop(0, 64 // batch, serve, 0)
     own_answer.start()
+    for_each(1, 8, lambda k: send_wo(k).start())
+    def gather(e, carry):
+        acc, weight = carry
+        s = scores[e]
+        w = jnp.where(s > 0.5 * NEG_FILL, jnp.exp(s - near_max), 0.0)
+        return acc + jnp.dot(w.astype(bf16), pages[e, :, 128:256], preferred_element_type=f32), weight + w
+
+    zero = jnp.zeros((32, 128), f32)
+    near, near_sum = lax.fori_loop(0, 64, gather, (zero, zero), unroll=8)
+    near_sum = jnp.sum(near_sum, axis=1, keepdims=True)
+
     own_answer.wait()
     for_each(1, 64, lambda k: answer(k).wait_recv())
 

time: 67.3 us -> 67.4 us (level)
  no operation moved by 1% of the time
where the time goes in v4:
time: 67.4 us; the launch traced here: 67.2 us
  Pallas kernels  65.9 us (98%)
  local copies, waits for them, and re-layouts  1.32 us (2%)
    pallas_call x1, Pallas kernels, shards(): pl.pallas_call(layer_kernel, out_shape=jax.ShapeDtypeStruct((64, 64), bf1...  65.9 us

profile of v4, /device:TPU:7, one launch (start us, length us, event | category | flops | bytes accessed | tf_op | source)
XLA Modules:
  0.0 67.2 jit_solution(16668813833665176376)
XLA Ops:
  0.0 65.9 %shard_map.82 = bf16[64,64]{1,0:T(8,128)(2,1)} custom-call(s32[64]{0:T(128)} %slots_ref.1, s32[8]{0:T(128)} %lengths_ref.1, s32[8,16]{1,0:T(8,128)} %table_ref.1, f32[8,128]{1,0:T(8,128)} %constant.2.clone.base_ref, bf16[64,512]{1,0:T(8,128)(2,1)} %bitcast.6, bf16[64,768]{1,0:T(8,128)(2,1)} %bitcast.5, bf16[64,512]{1,0:T(8,128)(2,1)} %bitcast.7, ...), custom_call_target="tpu_custom_call" | custom-call | tf_op jit(solution)/shard_map/pallas_call | solution.py:423
  65.9 1.3 %copy.10 = bf16[64,64]{1,0:T(8,128)(2,1)} copy(bf16[64,64]{1,0:T(8,128)(2,1)} %shard_map.82) | data formatting | bytes 16384

commit v5 on v4

--- a/solution.py
+++ b/solution.py
@@ -28,7 +28,8 @@
     def step(i, carry):
         body(i)
         return carry
-    lax.fori_loop(start, stop, step, 0)
+    unroll = {63: 7, 15: 5, 16: 4, 7: 7, 4: 4}.get(stop - start, 1)
+    lax.fori_loop(start, stop, step, 0, unroll=unroll)
 
 
 def place(req):
@@ -150,7 +151,7 @@
 
     def answer(k):
         peer = lax.rem(req - k + 64, 64)
-        return remote(reply.at[peer], back.at[req], s5.at[k], r5.at[k], peer)
+        return remote(reply.at[peer], back.at[req], s5.at[k], r5.at[0], peer)
 
     def send_rows(k):
         peer = x * 16 + lax.rem(y + k, 8) * 2 + c
@@ -257,22 +258,16 @@
     batch = 16
     row3 = lax.broadcasted_iota(jnp.int32, (batch, 8, 128), 1)
     lane3 = lax.broadcasted_iota(jnp.int32, (batch, 8, 128), 2)
-    own_answer = pltpu.make_async_copy(reply.at[req], back.at[req], own.at[0])
+    own_answer = pltpu.make_async_copy(reply.at[req], back.at[req], r5.at[0])
 
     def serve(j, carry):
         first = j * batch
 
-        def heard(k):
-            @pl.when(k > 0)
-            def _():
-                ask(k).wait_recv()
-
-        def tell(k):
-            @pl.when(k > 0)
-            def _():
-                answer(k).start()
-
-        for_each(first, first + batch, heard)
+        @pl.when(j > 0)
+        def _():
+            ask(first).wait_recv()
+
+        for_each(1, batch, lambda i: ask(first + i).wait_recv())
         sources = [lax.rem(req - first - i + 64, 64) for i in range(batch)]
         slots = [slots_ref[g] for g in sources]
         query, limit = [], []
@@ -297,7 +292,11 @@
                 w[i].astype(bf16), pages[slots[i], :, 128:256], preferred_element_type=f32
             )
             reply[sources[i]] = jnp.where(row < 4, a, stats[i]).astype(bf16)
-        for_each(first, first + batch, tell)
+        @pl.when(j > 0)
+        def _():
+            answer(first).start()
+
+        for_each(1, batch, lambda i: answer(first + i).start())
         return carry
 
     lax.fori_loop(0, 64 // batch, serve, 0)
@@ -313,8 +312,7 @@
     near, near_sum = lax.fori_loop(0, 64, gather, (zero, zero), unroll=8)
     near_sum = jnp.sum(near_sum, axis=1, keepdims=True)
 
-    own_answer.wait()
-    for_each(1, 64, lambda k: answer(k).wait_recv())
+    pltpu.make_async_copy(back, back, r5.at[0]).wait()
 
     far = back[...].astype(f32).reshape(512, 128).astype(bf16)
     pick_max = jnp.logical_and(lane < 48, lax.rem(lane, 16) == 0)
@@ -356,9 +354,11 @@
         [heads[:, 8 * q : 8 * q + 8].reshape(64, 128) for q in range(4)], axis=1
     ).astype(bf16)
     for i in range(8):
-        tile = dot_nt(heads, wide[i]).astype(bf16)
-        piece[2 * i] = tile[0:32]
-        piece[2 * i + 1] = tile[32:64]
+        tile = dot_nt(heads, wide[i])
+        for k in range(2):
+            piece[2 * i + k] = jnp.concatenate(
+                [tile[32 * k : 32 * k + 16], tile[32 * k + 16 : 32 * k + 32]], axis=1
+            ).astype(bf16)
 
     def send(k):
         @pl.when(is_me(dest(k)))
@@ -390,7 +390,7 @@
         total = pieces[8 * j].astype(f32)
         for h in range(1, 8):
             total = total + pieces[8 * j + h].astype(f32)
-        totals.append(total)
+        totals.append(jnp.concatenate([total[:, 0:64], total[:, 64:128]], axis=0))
     out_ref[...] = jnp.concatenate(
         [totals[j][8 * i : 8 * i + 8] for i in range(4) for j in range(2)], axis=0
     ).astype(bf16)
@@ -440,10 +440,10 @@
             pltpu.VMEM((64, 8, 128), bf16),
             pltpu.VMEM((32, 128), bf16),
             pltpu.VMEM((8, 32, 128), bf16),
-            pltpu.VMEM((16, 32, 64), bf16),
-            pltpu.VMEM((16, 32, 64), bf16),
+            pltpu.VMEM((16, 16, 128), bf16),
+            pltpu.VMEM((16, 16, 128), bf16),
             dma(4), dma(8), dma(8), dma(16), dma(16), dma(8), dma(8), dma(64), dma(64),
-            dma(64), dma(64), dma(8), dma(8), dma(16), dma(16),
+            dma(64), dma(1), dma(8), dma(8), dma(16), dma(16),
             dma(7), dma(8),
         ],
         compiler_params=params(1),

time: 67.4 us -> 62.1 us (0.921)
  Pallas kernels: 65.9 us -> 60.4 us
    pallas_call x1, Pallas kernels: 65.9 us -> 60.4 us  [shards(): pl.pallas_call(layer_kernel, out_shape=jax.ShapeDtypeStruct((64, 64), bf1...]
where the time goes in v5:
time: 62.1 us; the launch traced here: 61.7 us
  Pallas kernels  60.4 us (97%)
  local copies, waits for them, and re-layouts  1.32 us (2%)
    pallas_call x1, Pallas kernels, shards(): pl.pallas_call(layer_kernel, out_shape=jax.ShapeDtypeStruct((64, 64), bf1...  60.4 us
    unnamed x1, local copies, waits for them, and re-layouts  1.32 us

profile of v5, /device:TPU:7, one launch (start us, length us, event | category | flops | bytes accessed | tf_op | source)
XLA Modules:
  0.0 61.7 jit_solution(5816057251408851270)
XLA Ops:
  0.0 60.4 %shard_map.82 = bf16[64,64]{1,0:T(8,128)(2,1)} custom-call(s32[64]{0:T(128)} %slots_ref.1, s32[8]{0:T(128)} %lengths_ref.1, s32[8,16]{1,0:T(8,128)} %table_ref.1, f32[8,128]{1,0:T(8,128)} %constant.2.clone.base_ref, bf16[64,512]{1,0:T(8,128)(2,1)} %bitcast.6, bf16[64,768]{1,0:T(8,128)(2,1)} %bitcast.5, bf16[64,512]{1,0:T(8,128)(2,1)} %bitcast.7, ...), custom_call_target="tpu_custom_call" | custom-call | tf_op jit(solution)/shard_map/pallas_call | solution.py:423
  60.4 1.3 %copy.10 = bf16[64,64]{1,0:T(8,128)(2,1)} copy(bf16[64,64]{1,0:T(8,128)(2,1)} %shard_map.82) | data formatting | bytes 16384

commit v6 on v5

--- a/solution.py
+++ b/solution.py
@@ -28,7 +28,7 @@
     def step(i, carry):
         body(i)
         return carry
-    unroll = {63: 7, 15: 5, 16: 4, 7: 7, 4: 4}.get(stop - start, 1)
+    unroll = {63: 21, 15: 15, 16: 8, 7: 7, 4: 4}.get(stop - start, 1)
     lax.fori_loop(start, stop, step, 0, unroll=unroll)
 
 
@@ -147,11 +147,11 @@
 
     def ask(k):
         peer = lax.rem(req + k, 64)
-        return remote(ask_buf.at[peer], asked.at[req], s4.at[k], r4.at[k], peer)
+        return remote(ask_buf.at[peer], asked.at[req], s4.at[0], r4.at[k // 16], peer)
 
     def answer(k):
         peer = lax.rem(req - k + 64, 64)
-        return remote(reply.at[peer], back.at[req], s5.at[k], r5.at[0], peer)
+        return remote(reply.at[peer], back.at[req], s5.at[0], r5.at[0], peer)
 
     def send_rows(k):
         peer = x * 16 + lax.rem(y + k, 8) * 2 + c
@@ -238,7 +238,7 @@
         jnp.concatenate([queries, jnp.ones((8, 128), f32)], axis=0).astype(bf16),
     )
     ask_buf[...] = ask_rows.reshape(64, 8, 128).astype(bf16)
-    own_ask = pltpu.make_async_copy(ask_buf.at[req], asked.at[req], own.at[1])
+    own_ask = pltpu.make_async_copy(ask_buf.at[req], asked.at[req], r4.at[0])
     own_ask.start()
     for_each(1, 64, lambda k: ask(k).start())
     load.wait()
@@ -254,7 +254,6 @@
     near_max = lax.fori_loop(0, 64, score, jnp.full((32, 128), NEG_FILL, f32), unroll=8)
     near_max = jnp.max(near_max, axis=1, keepdims=True)
 
-    own_ask.wait()
     batch = 16
     row3 = lax.broadcasted_iota(jnp.int32, (batch, 8, 128), 1)
     lane3 = lax.broadcasted_iota(jnp.int32, (batch, 8, 128), 2)
@@ -263,11 +262,8 @@
     def serve(j, carry):
         first = j * batch
 
-        @pl.when(j > 0)
-        def _():
-            ask(first).wait_recv()
-
-        for_each(1, batch, lambda i: ask(first + i).wait_recv())
+        filled = asked.at[pl.ds(0, batch)]
+        pltpu.make_async_copy(filled, filled, r4.at[j]).wait()
         sources = [lax.rem(req - first - i + 64, 64) for i in range(batch)]
         slots = [slots_ref[g] for g in sources]
         query, limit = [], []
@@ -370,8 +366,9 @@
             push(k).start()
 
     for_each(0, 16, send)
-    for_each(1, 64, lambda k: ask(k).wait_send())
-    for_each(1, 64, lambda k: answer(k).wait_send())
+    for buffer, sem in ((ask_buf, s4.at[0]), (reply, s5.at[0])):
+        left = buffer.at[pl.ds(0, 63)]
+        pltpu.make_async_copy(left, left, sem).wait()
     for_each(1, 8, lambda k: send_pay(k).wait_send())
     for_each(0, 4, lambda k: send_w(k).wait_send())
     near_w().wait_send()
@@ -442,8 +439,8 @@
             pltpu.VMEM((8, 32, 128), bf16),
             pltpu.VMEM((16, 16, 128), bf16),
             pltpu.VMEM((16, 16, 128), bf16),
-            dma(4), dma(8), dma(8), dma(16), dma(16), dma(8), dma(8), dma(64), dma(64),
-            dma(64), dma(1), dma(8), dma(8), dma(16), dma(16),
+            dma(4), dma(8), dma(8), dma(16), dma(16), dma(8), dma(8), dma(1), dma(4),
+            dma(1), dma(1), dma(8), dma(8), dma(16), dma(16),
             dma(7), dma(8),
         ],
         compiler_params=params(1),

time: 62.1 us -> 60.1 us (0.968)
  Pallas kernels: 60.4 us -> 58.6 us
    pallas_call x1, Pallas kernels: 60.4 us -> 58.6 us  [shards(): pl.pallas_call(layer_kernel, out_shape=jax.ShapeDtypeStruct((64, 64), bf1...]
where the time goes in v6:
time: 60.1 us; the launch traced here: 59.9 us
  Pallas kernels  58.6 us (98%)
  local copies, waits for them, and re-layouts  1.32 us (2%)
    pallas_call x1, Pallas kernels, shards(): pl.pallas_call(layer_kernel, out_shape=jax.ShapeDtypeStruct((64, 64), bf1...  58.6 us
    unnamed x1, local copies, waits for them, and re-layouts  1.32 us

profile of v6, /device:TPU:7, one launch (start us, length us, event | category | flops | bytes accessed | tf_op | source)
XLA Modules:
  0.0 59.9 jit_solution(12981916363296370091)
XLA Ops:
  0.0 58.6 %shard_map.82 = bf16[64,64]{1,0:T(8,128)(2,1)} custom-call(s32[64]{0:T(128)} %slots_ref.1, s32[8]{0:T(128)} %lengths_ref.1, s32[8,16]{1,0:T(8,128)} %table_ref.1, f32[8,128]{1,0:T(8,128)} %constant.2.clone.base_ref, bf16[64,512]{1,0:T(8,128)(2,1)} %bitcast.6, bf16[64,768]{1,0:T(8,128)(2,1)} %bitcast.5, bf16[64,512]{1,0:T(8,128)(2,1)} %bitcast.7, ...), custom_call_target="tpu_custom_call" | custom-call | tf_op jit(solution)/shard_map/pallas_call | solution.py:420
  58.6 1.3 %copy.10 = bf16[64,64]{1,0:T(8,128)(2,1)} copy(bf16[64,64]{1,0:T(8,128)(2,1)} %shard_map.82) | data formatting | bytes 16384
